TPU v7x, 256 devices: a whole 4x4x8 slice. The times are simulated.
256 devices in a mesh: expert: 64 (over x, z, core), hidden: 4 (over y).
Axes of the slice: x: 4, y: 4, z: 8, core: 2. Of those that a mesh axis runs over, the one named last changes fastest.
Arguments:
- tokens: bfloat16 [1024, 7168], P('expert', 'hidden'), may hold values from -6 to 6
- routes: int32 [1024, 8], P('expert'), may hold values from 0 to 63, as said below
- combine: float32 [1024, 8], P('expert'), may hold values from 0.05 to 0.5
- w_gate: bfloat16 [64, 7168, 1024], P('expert', None, 'hidden'), may hold values from -0.0625 to 0.0625
- w_up: bfloat16 [64, 7168, 1024], P('expert', None, 'hidden'), may hold values from -0.0625 to 0.0625
- w_down: bfloat16 [64, 1024, 7168], P('expert', 'hidden'), may hold values from -0.1875 to 0.1875
- cotangent: bfloat16 [1024, 7168], P('expert', 'hidden'), may hold values from -6 to 6
Outputs:
- output: bfloat16 [1024, 7168], P('expert', 'hidden')
- grad_tokens: bfloat16 [1024, 7168], P('expert', 'hidden')
Inputs may be any that keep to these rules, and one draw needn't show every extreme that they name: `routes`: each row names 8 different experts. In each aligned block of 16 rows (the rows of one device) no expert is named by more than 4 rows, and the same expert is named by exactly 4 rows in every block.
All inputs are finite; a program needn't handle non-finite values.
Results may differ from a plain program's by a relative error of at most 0.012.
Values may be sent and summed in bfloat16 or wider, within the bound.
No kernel may reach another device: no remote copies, remote signals or barrier semaphores. Data moves between devices by JAX's collectives and lax.ppermute only.
A program may use at most 128 MiB of HBM per device.

v0:
```python
import jax
import jax.numpy as jnp
from jax import lax
from jax.sharding import PartitionSpec as P


def per_device(tokens, routes, combine, w_gate, w_up, w_down, cotangent):
    tok_rows = tokens.shape[0]
    top_count = routes.shape[1]
    local_experts = w_gate.shape[0]
    sources = lax.axis_size("expert")
    experts = local_experts * sources
    pair_count = tok_rows * top_count
    capacity = 2 * pair_count // experts
    flat_routes = routes.reshape(pair_count)
    onehot = (flat_routes[:, None] == jnp.arange(experts, dtype=jnp.int32)[None, :]).astype(
        jnp.int32
    )
    slot_rank = jnp.sum((jnp.cumsum(onehot, axis=0) - 1) * onehot, axis=1)
    target = flat_routes * capacity + slot_rank
    slot_table = (
        jnp.full((experts * capacity,), pair_count, jnp.int32)
        .at[target]
        .set(jnp.arange(pair_count, dtype=jnp.int32))
    )
    source_rows = slot_table // top_count

    def pack_rows(values):
        padded = jnp.concatenate([values, jnp.zeros((1, values.shape[1]), values.dtype)], axis=0)
        return padded[source_rows].reshape(experts, capacity, values.shape[1])

    def to_local(arrived):
        columns = arrived.shape[2]
        sectioned = arrived.reshape(sources, local_experts, capacity, columns).transpose(1, 0, 2, 3)
        return sectioned.reshape(local_experts, sources * capacity, columns)

    def to_global(leaving):
        columns = leaving.shape[2]
        sectioned = leaving.reshape(local_experts, sources, capacity, columns).transpose(1, 0, 2, 3)
        return sectioned.reshape(experts, capacity, columns)

    def unpack(returned):
        flattened = returned.reshape(experts * capacity, returned.shape[2])
        picked = (
            flattened[target].astype(jnp.float32).reshape(tok_rows, top_count, returned.shape[2])
        )
        return jnp.sum(picked * combine[:, :, None], axis=1).astype(jnp.bfloat16)

    full_tokens, full_grads = (
        lax.all_gather(tokens, "hidden", axis=1, tiled=True),
        lax.all_gather(cotangent, "hidden", axis=1, tiled=True),
    )
    arrived_x, arrived_dy = (
        lax.all_to_all(pack_rows(full_tokens), "expert", split_axis=0, concat_axis=0, tiled=True),
        lax.all_to_all(pack_rows(full_grads), "expert", split_axis=0, concat_axis=0, tiled=True),
    )
    arrived_x = to_local(arrived_x)
    arrived_dy = to_local(arrived_dy)
    gate_pre = jnp.einsum("erd,edf->erf", arrived_x, w_gate, preferred_element_type=jnp.float32)
    up_pre = jnp.einsum("erd,edf->erf", arrived_x, w_up, preferred_element_type=jnp.float32)
    back_hidden = jnp.einsum("erd,efd->erf", arrived_dy, w_down, preferred_element_type=jnp.float32)
    sigmoid_gate = jax.nn.sigmoid(gate_pre)
    activated = gate_pre * sigmoid_gate
    hidden_act = (activated * up_pre).astype(jnp.bfloat16)
    out_terms = jnp.einsum(
        "erf,efd->erd", hidden_act, w_down, preferred_element_type=jnp.float32
    ).astype(jnp.bfloat16)
    grad_gate = (
        back_hidden * up_pre * sigmoid_gate * (1.0 + gate_pre * (1.0 - sigmoid_gate))
    ).astype(jnp.bfloat16)
    grad_up = (back_hidden * activated).astype(jnp.bfloat16)
    out_share = (
        lax.psum_scatter(out_terms, "hidden", scatter_dimension=2, tiled=True)
        .astype(jnp.float32)
        .astype(jnp.bfloat16)
    )
    out_back = lax.all_to_all(
        to_global(out_share), "expert", split_axis=0, concat_axis=0, tiled=True
    )
    grad_terms = jnp.einsum("erf,edf->erd", grad_gate, w_gate, preferred_element_type=jnp.float32)
    grad_terms = grad_terms + jnp.einsum(
        "erf,edf->erd", grad_up, w_up, preferred_element_type=jnp.float32
    )
    grad_share = lax.psum_scatter(
        grad_terms.astype(jnp.bfloat16), "hidden", scatter_dimension=2, tiled=True
    )
    grad_back = lax.all_to_all(
        to_global(grad_share), "expert", split_axis=0, concat_axis=0, tiled=True
    )
    return (unpack(out_back), unpack(grad_back))


def solution(mesh):
    return jax.shard_map(
        per_device,
        mesh=mesh,
        in_specs=(
            P("expert", "hidden"),
            P("expert", None),
            P("expert", None),
            P("expert", None, "hidden"),
            P("expert", None, "hidden"),
            P("expert", "hidden", None),
            P("expert", "hidden"),
        ),
        out_specs=(P("expert", "hidden"), P("expert", "hidden")),
        check_vma=False,
    )
```

profile of v0, /device:TPU:1, one launch (start us, length us, event | category | flops | bytes accessed | tf_op | source)
XLA Modules:
  0.0 376.7 jit_solution(7384329820560106243)
XLA Ops:
  7.2 0.8 copy.13
  7.9 0.7 broadcast_multiply_fusion
  8.6 0.1 eq.15
  8.7 0.1 fusion.17
  8.8 0.2 reduce_window_sum.11
  9.0 0.2 select_reduce_fusion
  9.1 0.1 copy.12
  9.2 0.1 mul.63
  9.3 1.0 scatter_custom_fusion
  10.3 11.0 %all_gather.6 = bf16[16,7168]{1,0:T(8,128)(2,1)S(1)} all-gather(bf16[16,1792]{1,0:T(8,128)(2,1)} %param.7), channel_id=1, replica_groups=mesh['expert'=64,'hidden'=4] {'hidden'}, dimensions={1}, use_global_device_ids=true | all-gather | bytes 286720 | tf_op jit(solution)/shard_map/all_gather | solution.py:50
  21.4 4.7 %gather_fusion = bf16[256,7168]{1,0:T(8,128)(2,1)} fusion(bf16[17,7168]{1,0:T(8,128)(2,1)S(1)} %concatenate.6, s32[1024]{0:T(1024)S(1)} %pad_clamp_fusion.1), kind=kCustom, calls=%fused_computation | custom fusion | bytes 7341056 | tf_op jit(solution)/shard_map/gather | solution.py:30
  26.1 7.0 %reshape.108 = bf16[64,4,7168]{2,1,0:T(4,128)(2,1)} reshape(bf16[256,7168]{1,0:T(8,128)(2,1)} %gather_fusion) | data formatting | bytes 7340032 | tf_op jit(solution)/shard_map/reshape | solution.py:30
  33.1 15.2 %all-to-all-start = ((bf16[64,4,7168]{2,1,0:T(4,128)(2,1)}), bf16[64,4,7168]{2,1,0:T(4,128)(2,1)}, u32[]{:S(2)}, u32[]{:S(2)}) async-start(bf16[64,4,7168]{2,1,0:T(4,128)(2,1)} %reshape.108), calls=%async_computation | async-start | bytes 7340032 | tf_op jit(solution)/shard_map/all_to_all | solution.py:54
  48.2 10.5 %all_gather.7 = bf16[16,7168]{1,0:T(8,128)(2,1)S(1)} all-gather(bf16[16,1792]{1,0:T(8,128)(2,1)S(1)} %copy-done.4), channel_id=1, replica_groups=mesh['expert'=64,'hidden'=4] {'hidden'}, dimensions={1}, use_global_device_ids=true | all-gather | bytes 286720 | tf_op jit(solution)/shard_map/all_gather | solution.py:51
  58.8 4.8 %gather_fusion.2 = bf16[256,7168]{1,0:T(8,128)(2,1)} fusion(bf16[17,7168]{1,0:T(8,128)(2,1)S(1)} %concatenate.7, s32[1024]{0:T(1024)S(1)} %pad_clamp_fusion.1), kind=kCustom, calls=%fused_computation.2 | custom fusion | bytes 7341056 | tf_op jit(solution)/shard_map/gather | solution.py:30
  63.6 7.0 %reshape.114 = bf16[64,4,7168]{2,1,0:T(4,128)(2,1)} reshape(bf16[256,7168]{1,0:T(8,128)(2,1)} %gather_fusion.2) | data formatting | bytes 7340032 | tf_op jit(solution)/shard_map/reshape | solution.py:30
  70.6 62.3 %all-to-all-done = bf16[64,4,7168]{2,1,0:T(4,128)(2,1)} async-done(((bf16[64,4,7168]{2,1,0:T(4,128)(2,1)}), bf16[64,4,7168]{2,1,0:T(4,128)(2,1)}, u32[]{:S(2)}, u32[]{:S(2)}) %all-to-all-start) | async-done | bytes 3670048 | tf_op jit(solution)/shard_map/all_to_all | solution.py:54
  132.9 5.9 %all-to-all-start.2 = ((bf16[64,4,7168]{2,1,0:T(4,128)(2,1)}), bf16[64,4,7168]{2,1,0:T(4,128)(2,1)}, u32[]{:S(2)}, u32[]{:S(2)}) async-start(bf16[64,4,7168]{2,1,0:T(4,128)(2,1)} %reshape.114), calls=%async_computation.3 | async-start | bytes 7340032 | tf_op jit(solution)/shard_map/all_to_all | solution.py:55
  138.8 0.2 reduce-scatter.5.cloned.1.call-start
  139.0 6.7 %reshape.109 = bf16[256,7168]{1,0:T(8,128)(2,1)} reshape(bf16[64,4,7168]{2,1,0:T(4,128)(2,1)} %all-to-all-done) | data formatting | bytes 7340032 | tf_op jit(solution)/shard_map/reshape
  145.8 4.4 %fusion.11 = f32[256,256]{1,0:T(8,128)S(1)} fusion(bf16[256,7168]{1,0:T(8,128)(2,1)} %reshape.109, bf16[1,7168,256]{2,1,0:T(8,128)(2,1)} %param.10), kind=kOutput, calls=%fused_computation.18 | convolution fusion | flops 939524096 | bytes 7602176 | tf_op jit(solution)/shard_map/erd,edf->erf/dot_general | solution.py:59
  150.2 0.9 copy-done.2
  151.1 1.1 fusion.7
  152.2 71.3 %all-to-all-done.2 = bf16[64,4,7168]{2,1,0:T(4,128)(2,1)} async-done(((bf16[64,4,7168]{2,1,0:T(4,128)(2,1)}), bf16[64,4,7168]{2,1,0:T(4,128)(2,1)}, u32[]{:S(2)}, u32[]{:S(2)}) %all-to-all-start.2) | async-done | bytes 3670048 | tf_op jit(solution)/shard_map/all_to_all | solution.py:55
  223.4 6.7 %reshape.115 = bf16[256,7168]{1,0:T(8,128)(2,1)} reshape(bf16[64,4,7168]{2,1,0:T(4,128)(2,1)} %all-to-all-done.2) | data formatting | bytes 7340032 | tf_op jit(solution)/shard_map/reshape.19
  230.2 4.4 %fusion.3 = f32[256,256]{1,0:T(8,128)S(1)} fusion(bf16[256,7168]{1,0:T(8,128)(2,1)} %reshape.115, bf16[1,256,7168]{2,1,0:T(8,128)(2,1)} %param.12), kind=kOutput, calls=%fused_computation.10 | convolution fusion | flops 939524096 | bytes 7602176 | tf_op jit(solution)/shard_map/erd,efd->erf/dot_general | solution.py:61
  234.6 0.0 copy-start.3
  234.6 1.2 fusion.9
  235.8 0.9 copy-done.3
  236.7 3.0 fusion.2
  239.7 0.0 reduce-scatter.5.cloned.1.call-update
  239.7 0.0 reduce-scatter.3.cloned.1.call-start
  239.7 5.0 %fusion.1 = bf16[1,256,7168]{2,1,0:T(8,128)(2,1)} fusion(bf16[1,256,7168]{2,1,0:T(8,128)(2,1)} %param.12, f32[256,256]{1,0:T(8,128)S(1)} %fusion.7, f32[256,256]{1,0:T(8,128)S(1)} %fusion.11), kind=kOutput, calls=%fused_computation.8 | convolution fusion | flops 941752320 | bytes 7864320 | tf_op jit(solution)/shard_map/erf,efd->erd/dot_general | solution.py:65
  244.7 0.0 reduce-scatter.3.cloned.1.call-update
  244.7 0.0 copy-start.5
  244.7 36.1 %reduce-scatter.5.cloned.1.call-done = bf16[1,256,1792]{2,1,0:T(8,128)(2,1)} async-done(((bf16[1,256,7168]{2,1,0:T(8,128)(2,1)}), bf16[1,256,1792]{2,1,0:T(8,128)(2,1)}) %reduce-scatter.5.cloned.1.call-update) | async-done | bytes 917520 | tf_op jit(solution)/shard_map/reduce_scatter | solution.py:84
  280.8 2.5 reshape_transpose_reshape.9
  283.3 10.7 %all-to-all-start.3 = ((bf16[64,4,1792]{2,1,0:T(4,128)(2,1)}), bf16[64,4,1792]{2,1,0:T(4,128)(2,1)S(1)}, u32[]{:S(2)}, u32[]{:S(2)}) async-start(bf16[64,4,1792]{2,1,0:T(4,128)(2,1)} %reshape_transpose_reshape.9), calls=%async_computation.5 | async-start | bytes 1835008 | tf_op jit(solution)/shard_map/all_to_all | solution.py:87
  294.1 34.2 %reduce-scatter.3.cloned.1.call-done = bf16[1,256,1792]{2,1,0:T(8,128)(2,1)} async-done(((bf16[1,256,7168]{2,1,0:T(8,128)(2,1)}), bf16[1,256,1792]{2,1,0:T(8,128)(2,1)}) %reduce-scatter.3.cloned.1.call-update) | async-done | bytes 917520 | tf_op jit(solution)/shard_map/reduce_scatter | solution.py:73
  328.3 2.5 reshape_transpose_reshape.8
  330.8 10.7 %all-to-all-start.1 = ((bf16[64,4,1792]{2,1,0:T(4,128)(2,1)}), bf16[64,4,1792]{2,1,0:T(4,128)(2,1)S(1)}, u32[]{:S(2)}, u32[]{:S(2)}) async-start(bf16[64,4,1792]{2,1,0:T(4,128)(2,1)} %reshape_transpose_reshape.8), calls=%async_computation.2 | async-start | bytes 1835008 | tf_op jit(solution)/shard_map/all_to_all | solution.py:77
  341.6 0.1 copy.14
  341.6 0.2 reshape.116
  341.9 0.9 gather_fusion.3
  342.8 24.5 %all-to-all-done.1 = bf16[64,4,1792]{2,1,0:T(4,128)(2,1)S(1)} async-done(((bf16[64,4,1792]{2,1,0:T(4,128)(2,1)}), bf16[64,4,1792]{2,1,0:T(4,128)(2,1)S(1)}, u32[]{:S(2)}, u32[]{:S(2)}) %all-to-all-start.1) | async-done | bytes 917536 | tf_op jit(solution)/shard_map/all_to_all | solution.py:77
  367.3 0.2 reshape.113
  367.5 0.9 gather_fusion.1
  368.4 1.4 fusion.13
  (16 shorter events, 0.1 us)
Async XLA Ops:
  33.1 15.2 %copy-start.4 = (bf16[16,1792]{1,0:T(8,128)(2,1)S(1)}, bf16[16,1792]{1,0:T(8,128)(2,1)}, u32[]{:S(2)}) copy-start(bf16[16,1792]{1,0:T(8,128)(2,1)} %param.13) | copy-start | bytes 172036
  33.1 99.8 %all-to-all-start = ((bf16[64,4,7168]{2,1,0:T(4,128)(2,1)}), bf16[64,4,7168]{2,1,0:T(4,128)(2,1)}, u32[]{:S(2)}, u32[]{:S(2)}) async-start(bf16[64,4,7168]{2,1,0:T(4,128)(2,1)} %reshape.108), calls=%async_computation | async-start | bytes 7340032 | tf_op jit(solution)/shard_map/all_to_all | solution.py:54
  132.9 90.6 %all-to-all-start.2 = ((bf16[64,4,7168]{2,1,0:T(4,128)(2,1)}), bf16[64,4,7168]{2,1,0:T(4,128)(2,1)}, u32[]{:S(2)}, u32[]{:S(2)}) async-start(bf16[64,4,7168]{2,1,0:T(4,128)(2,1)} %reshape.114), calls=%async_computation.3 | async-start | bytes 7340032 | tf_op jit(solution)/shard_map/all_to_all | solution.py:55
  138.8 142.0 %reduce-scatter.5.cloned.1.call-start = ((), (), s32[]{:S(2)}) async-start(), calls=%async_computation.7 | async-start | bytes 4587520 | tf_op jit(solution)/shard_map/reduce_scatter | solution.py:84
  145.8 4.4 %copy-start = (bf16[256,7168]{1,0:T(8,128)(2,1)S(1)}, bf16[256,7168]{1,0:T(8,128)(2,1)}, u32[]{:S(2)}) copy-start(bf16[256,7168]{1,0:T(8,128)(2,1)} %reshape.109) | copy-start | bytes 11010052
  145.8 5.3 %copy-start.2 = (bf16[1,7168,256]{2,1,0:T(8,128)(2,1)S(1)}, bf16[1,7168,256]{2,1,0:T(8,128)(2,1)}, u32[]{:S(2)}) copy-start(bf16[1,7168,256]{2,1,0:T(8,128)(2,1)} %param.11) | copy-start | bytes 11010052
  230.2 4.5 %copy-start.1 = (bf16[1,7168,256]{2,1,0:T(8,128)(2,1)S(1)}, bf16[1,7168,256]{2,1,0:T(8,128)(2,1)}, u32[]{:S(2)}) copy-start(bf16[1,7168,256]{2,1,0:T(8,128)(2,1)} %param.10) | copy-start | bytes 11010052
  234.6 2.0 copy-start.3
  239.7 88.6 %reduce-scatter.3.cloned.1.call-start = ((), (), s32[]{:S(2)}) async-start(), calls=%async_computation.6 | async-start | bytes 4587520 | tf_op jit(solution)/shard_map/reduce_scatter | solution.py:73
  244.7 96.8 %copy-start.5 = (f32[16,8]{0,1:T(8,128)S(1)}, f32[16,8]{0,1:T(8,128)}, u32[]{:S(2)}) copy-start(f32[16,8]{0,1:T(8,128)} %param.9) | copy-start | bytes 1540
  283.3 47.5 %all-to-all-start.3 = ((bf16[64,4,1792]{2,1,0:T(4,128)(2,1)}), bf16[64,4,1792]{2,1,0:T(4,128)(2,1)S(1)}, u32[]{:S(2)}, u32[]{:S(2)}) async-start(bf16[64,4,1792]{2,1,0:T(4,128)(2,1)} %reshape_transpose_reshape.9), calls=%async_computation.5 | async-start | bytes 1835008 | tf_op jit(solution)/shard_map/all_to_all | solution.py:87
  330.8 36.5 %all-to-all-start.1 = ((bf16[64,4,1792]{2,1,0:T(4,128)(2,1)}), bf16[64,4,1792]{2,1,0:T(4,128)(2,1)S(1)}, u32[]{:S(2)}, u32[]{:S(2)}) async-start(bf16[64,4,1792]{2,1,0:T(4,128)(2,1)} %reshape_transpose_reshape.8), calls=%async_computation.2 | async-start | bytes 1835008 | tf_op jit(solution)/shard_map/all_to_all | solution.py:77
Sparse Core Ops, SparseCore 0:
  239.8 40.9 reduce-scatter.4
  283.4 44.8 reduce-scatter.2
where the time goes:
time: 378 us; the launch traced here: 377 us
  waiting for transfers between devices  228 us (60%)
  local copies, waits for them, and re-layouts  48.1 us (13%)
  starting transfers between devices  42.8 us (11%)
  blocking collectives  21.5 us (6%)
  matrix products  19.1 us (5%)
  between operations  14.2 us (4%)
    all_to_all x1, waiting for transfers between devices, per_device(): lax.all_to_all(pack_rows(full_grads), 'expert', split_axis=0, concat_axis...  71.3 us
    all_to_all x1, waiting for transfers between devices, per_device(): lax.all_to_all(pack_rows(full_tokens), 'expert', split_axis=0, concat_axi...  62.3 us
    reduce_scatter x1, waiting for transfers between devices, per_device(): lax.psum_scatter(grad_terms.astype(jnp.bfloat16), 'hidden', scatter_dimen...  36.1 us
    reduce_scatter x1, waiting for transfers between devices, per_device(): lax.psum_scatter(out_terms, 'hidden', scatter_dimension=2, tiled=True)  34.2 us
    all_to_all x1, waiting for transfers between devices, per_device(): lax.all_to_all(to_global(out_share), 'expert', split_axis=0, concat_axis=...  24.5 us
    all_to_all x1, starting transfers between devices, per_device(): lax.all_to_all(pack_rows(full_tokens), 'expert', split_axis=0, concat_axi...  15.2 us
    reshape x2, local copies, waits for them, and re-layouts, pack_rows(): return padded[source_rows].reshape(experts, capacity, values.shape[1])  14 us
    all_gather x1, blocking collectives, per_device(): lax.all_gather(tokens, 'hidden', axis=1, tiled=True)  11 us
  transfers between devices with their start and end apart: 6, of which 5 were waited for; matrix products, arithmetic and copies ran while one was open for 9% of the time, Pallas kernels for 0%

commit v1 on v0

--- a/solution.py
+++ b/solution.py
@@ -2,6 +2,7 @@
 import jax.numpy as jnp
 from jax import lax
 from jax.sharding import PartitionSpec as P
+from jax.lax import all_to_all, psum
 
 
 def per_device(tokens, routes, combine, w_gate, w_up, w_down, cotangent):
@@ -46,9 +47,15 @@
         )
         return jnp.sum(picked * combine[:, :, None], axis=1).astype(jnp.bfloat16)
 
+    def derive_packet(v0, named_axis):
+        a_next = jnp.concatenate(
+            all_to_all(jnp.stack([v0] * psum(1, named_axis), axis=0), named_axis, 0, 0), axis=1
+        )
+        return a_next
+
     full_tokens, full_grads = (
         lax.all_gather(tokens, "hidden", axis=1, tiled=True),
-        lax.all_gather(cotangent, "hidden", axis=1, tiled=True),
+        derive_packet(cotangent, "hidden"),
     )
     arrived_x, arrived_dy = (
         lax.all_to_all(pack_rows(full_tokens), "expert", split_axis=0, concat_axis=0, tiled=True),

time: 378 us -> 337 us (0.89)
  waiting for transfers between devices: 228 us -> 198 us
  blocking collectives: 21.5 us -> 10.1 us
    reduce_scatter x1, waiting for transfers between devices: 34.2 us -> 0.02 us  [per_device(): lax.psum_scatter(out_terms, 'hidden', scatter_dimension=2, tiled=True)]
    all_to_all x1, waiting for transfers between devices: 24.5 us -> 0.01 us  [per_device(): lax.all_to_all(to_global(out_share), 'expert', split_axis=0, concat_axis=...]
    all_to_all x1, waiting for transfers between devices: 0.01 us -> 24.5 us  [per_device(): lax.all_to_all(to_global(grad_share), 'expert', split_axis=0, concat_axis...]
    all_to_all x1, waiting for transfers between devices: 62.3 us -> 72.8 us  [per_device(): lax.all_to_all(pack_rows(full_tokens), 'expert', split_axis=0, concat_axi...]
    all_gather x1 -> x0, blocking collectives: 10.5 us -> none  [per_device(): lax.all_gather(cotangent, 'hidden', axis=1, tiled=True)]
    all_to_all x0 -> x1, starting transfers between devices: none -> 5 us  [derive_packet(): all_to_all(jnp.stack([v0] * psum(1, named_axis), axis=0), named_axis, 0, 0)]
    all_to_all x1, starting transfers between devices: 10.7 us -> 5.74 us  [per_device(): lax.all_to_all(to_global(out_share), 'expert', split_axis=0, concat_axis=...]
    all_to_all x1, waiting for transfers between devices: 71.3 us -> 67.2 us  [per_device(): lax.all_to_all(pack_rows(full_grads), 'expert', split_axis=0, concat_axis...]
  transfers between devices with their start and end apart: 6 -> 7, of which waited for: 5 -> 4; matrix products, arithmetic and copies ran while one was open for 9% -> 19% of each run, Pallas kernels for 0% -> 0%
where the time goes in v1:
time: 337 us; the launch traced here: 335 us
  waiting for transfers between devices  198 us (59%)
  local copies, waits for them, and re-layouts  50.5 us (15%)
  starting transfers between devices  43.4 us (13%)
  matrix products  17.1 us (5%)
  between operations  14.2 us (4%)
  blocking collectives  10.1 us (3%)
    all_to_all x1, waiting for transfers between devices, per_device(): lax.all_to_all(pack_rows(full_tokens), 'expert', split_axis=0, concat_axi...  72.8 us
    all_to_all x1, waiting for transfers between devices, per_device(): lax.all_to_all(pack_rows(full_grads), 'expert', split_axis=0, concat_axis...  67.2 us
    reduce_scatter x1, waiting for transfers between devices, per_device(): lax.psum_scatter(grad_terms.astype(jnp.bfloat16), 'hidden', scatter_dimen...  32.9 us
    all_to_all x1, waiting for transfers between devices, per_device(): lax.all_to_all(to_global(grad_share), 'expert', split_axis=0, concat_axis...  24.5 us
    all_to_all x1, starting transfers between devices, per_device(): lax.all_to_all(pack_rows(full_tokens), 'expert', split_axis=0, concat_axi...  15.8 us
    reshape x2, local copies, waits for them, and re-layouts, pack_rows(): return padded[source_rows].reshape(experts, capacity, values.shape[1])  14 us
    all_to_all x1, starting transfers between devices, per_device(): lax.all_to_all(to_global(grad_share), 'expert', split_axis=0, concat_axis...  10.7 us
    all_gather x1, blocking collectives, per_device(): lax.all_gather(tokens, 'hidden', axis=1, tiled=True)  10.1 us
  transfers between devices with their start and end apart: 7, of which 4 were waited for; matrix products, arithmetic and copies ran while one was open for 19% of the time, Pallas kernels for 0%

profile of v1, /device:TPU:1, one launch (start us, length us, event | category | flops | bytes accessed | tf_op | source)
XLA Modules:
  0.0 335.5 jit_solution(4621534965380974733)
XLA Ops:
  7.2 1.5 stack.2
  8.7 5.0 %all-to-all-start.2 = ((bf16[4,16,1792]{2,1,0:T(8,128)(2,1)}), bf16[4,16,1792]{2,1,0:T(8,128)(2,1)S(1)}, u32[]{:S(2)}, u32[]{:S(2)}) async-start(bf16[4,16,1792]{2,1,0:T(8,128)(2,1)} %stack.2), calls=%async_computation.3 | async-start | bytes 458752 | tf_op jit(solution)/shard_map/all_to_all | solution.py:52
  13.7 0.8 copy.16
  14.4 0.7 broadcast_multiply_fusion
  15.1 0.1 eq.15
  15.2 0.1 fusion.17
  15.3 0.2 reduce_window_sum.11
  15.5 0.2 select_reduce_fusion
  15.7 0.1 copy.15
  15.7 0.1 mul.63
  15.9 1.0 scatter_custom_fusion
  16.9 10.1 %all_gather.3 = bf16[16,7168]{1,0:T(8,128)(2,1)S(1)} all-gather(bf16[16,1792]{1,0:T(8,128)(2,1)} %param.7), channel_id=1, replica_groups=mesh['expert'=64,'hidden'=4] {'hidden'}, dimensions={1}, use_global_device_ids=true | all-gather | bytes 286720 | tf_op jit(solution)/shard_map/all_gather | solution.py:57
  27.0 4.7 %gather_fusion = bf16[256,7168]{1,0:T(8,128)(2,1)} fusion(bf16[17,7168]{1,0:T(8,128)(2,1)S(1)} %concatenate.6, s32[1024]{0:T(1024)S(1)} %pad_clamp_fusion.1), kind=kCustom, calls=%fused_computation | custom fusion | bytes 7341056 | tf_op jit(solution)/shard_map/gather | solution.py:31
  31.6 7.0 %reshape.116 = bf16[64,4,7168]{2,1,0:T(4,128)(2,1)} reshape(bf16[256,7168]{1,0:T(8,128)(2,1)} %gather_fusion) | data formatting | bytes 7340032 | tf_op jit(solution)/shard_map/reshape | solution.py:31
  38.7 15.8 %all-to-all-start = ((bf16[64,4,7168]{2,1,0:T(4,128)(2,1)}), bf16[64,4,7168]{2,1,0:T(4,128)(2,1)}, u32[]{:S(2)}, u32[]{:S(2)}) async-start(bf16[64,4,7168]{2,1,0:T(4,128)(2,1)} %reshape.116), calls=%async_computation | async-start | bytes 7340032 | tf_op jit(solution)/shard_map/all_to_all | solution.py:61
  54.5 4.8 %gather_fusion.2 = bf16[256,7168]{1,0:T(8,128)(2,1)} fusion(bf16[17,7168]{1,0:T(8,128)(2,1)S(1)} %concatenate.7, s32[1024]{0:T(1024)S(1)} %pad_clamp_fusion.1), kind=kCustom, calls=%fused_computation.2 | custom fusion | bytes 7341056 | tf_op jit(solution)/shard_map/gather | solution.py:31
  59.2 7.0 %reshape.124 = bf16[64,4,7168]{2,1,0:T(4,128)(2,1)} reshape(bf16[256,7168]{1,0:T(8,128)(2,1)} %gather_fusion.2) | data formatting | bytes 7340032 | tf_op jit(solution)/shard_map/reshape | solution.py:31
  66.2 72.8 %all-to-all-done = bf16[64,4,7168]{2,1,0:T(4,128)(2,1)} async-done(((bf16[64,4,7168]{2,1,0:T(4,128)(2,1)}), bf16[64,4,7168]{2,1,0:T(4,128)(2,1)}, u32[]{:S(2)}, u32[]{:S(2)}) %all-to-all-start) | async-done | bytes 3670048 | tf_op jit(solution)/shard_map/all_to_all | solution.py:61
  139.1 5.9 %all-to-all-start.3 = ((bf16[64,4,7168]{2,1,0:T(4,128)(2,1)}), bf16[64,4,7168]{2,1,0:T(4,128)(2,1)}, u32[]{:S(2)}, u32[]{:S(2)}) async-start(bf16[64,4,7168]{2,1,0:T(4,128)(2,1)} %reshape.124), calls=%async_computation.4 | async-start | bytes 7340032 | tf_op jit(solution)/shard_map/all_to_all | solution.py:62
  145.0 0.2 reduce-scatter.3.cloned.1.call-start
  145.2 6.7 %reshape.117 = bf16[256,7168]{1,0:T(8,128)(2,1)} reshape(bf16[64,4,7168]{2,1,0:T(4,128)(2,1)} %all-to-all-done) | data formatting | bytes 7340032 | tf_op jit(solution)/shard_map/reshape
  151.9 4.4 %fusion.11 = f32[256,256]{1,0:T(8,128)S(1)} fusion(bf16[256,7168]{1,0:T(8,128)(2,1)} %reshape.117, bf16[1,7168,256]{2,1,0:T(8,128)(2,1)} %param.10), kind=kOutput, calls=%fused_computation.18 | convolution fusion | flops 939524096 | bytes 7602176 | tf_op jit(solution)/shard_map/erd,edf->erf/dot_general | solution.py:66
  156.4 0.9 copy-done.3
  157.2 1.1 fusion.7
  158.4 0.9 copy-done.1
  159.3 3.0 fusion.1
  162.3 0.0 reduce-scatter.3.cloned.1.call-update
  162.3 0.0 reduce-scatter.5.cloned.1.call-start
  162.4 67.2 %all-to-all-done.3 = bf16[64,4,7168]{2,1,0:T(4,128)(2,1)} async-done(((bf16[64,4,7168]{2,1,0:T(4,128)(2,1)}), bf16[64,4,7168]{2,1,0:T(4,128)(2,1)}, u32[]{:S(2)}, u32[]{:S(2)}) %all-to-all-start.3) | async-done | bytes 3670048 | tf_op jit(solution)/shard_map/all_to_all | solution.py:62
  229.6 6.7 %reshape.125 = bf16[256,7168]{1,0:T(8,128)(2,1)} reshape(bf16[64,4,7168]{2,1,0:T(4,128)(2,1)} %all-to-all-done.3) | data formatting | bytes 7340032 | tf_op jit(solution)/shard_map/reshape.22
  236.4 4.4 %fusion.3 = f32[256,256]{1,0:T(8,128)S(1)} fusion(bf16[256,7168]{1,0:T(8,128)(2,1)} %reshape.125, bf16[1,256,7168]{2,1,0:T(8,128)(2,1)} %param.12), kind=kOutput, calls=%fused_computation.10 | convolution fusion | flops 939524096 | bytes 7602176 | tf_op jit(solution)/shard_map/erd,efd->erf/dot_general | solution.py:68
  240.8 1.2 fusion.9
  242.0 0.9 copy-done.4
  242.9 2.9 fusion.2
  245.8 0.0 reduce-scatter.5.cloned.1.call-update
  245.8 0.0 reduce-scatter.3.cloned.1.call-done
  245.9 2.5 reshape_transpose_reshape.8
  248.4 5.7 %all-to-all-start.1 = ((bf16[64,4,1792]{2,1,0:T(4,128)(2,1)}), bf16[64,4,1792]{2,1,0:T(4,128)(2,1)S(1)}, u32[]{:S(2)}, u32[]{:S(2)}) async-start(bf16[64,4,1792]{2,1,0:T(4,128)(2,1)} %reshape_transpose_reshape.8), calls=%async_computation.2 | async-start | bytes 1835008 | tf_op jit(solution)/shard_map/all_to_all | solution.py:84
  254.2 32.9 %reduce-scatter.5.cloned.1.call-done = bf16[1,256,1792]{2,1,0:T(8,128)(2,1)} async-done(((bf16[1,256,7168]{2,1,0:T(8,128)(2,1)}), bf16[1,256,1792]{2,1,0:T(8,128)(2,1)}) %reduce-scatter.5.cloned.1.call-update) | async-done | bytes 917520 | tf_op jit(solution)/shard_map/reduce_scatter | solution.py:91
  287.1 2.5 reshape_transpose_reshape.9
  289.6 10.7 %all-to-all-start.4 = ((bf16[64,4,1792]{2,1,0:T(4,128)(2,1)}), bf16[64,4,1792]{2,1,0:T(4,128)(2,1)S(1)}, u32[]{:S(2)}, u32[]{:S(2)}) async-start(bf16[64,4,1792]{2,1,0:T(4,128)(2,1)} %reshape_transpose_reshape.9), calls=%async_computation.6 | async-start | bytes 1835008 | tf_op jit(solution)/shard_map/all_to_all | solution.py:94
  300.3 0.1 copy.17
  300.4 0.2 reshape.121
  300.6 0.9 gather_fusion.1
  301.5 24.5 %all-to-all-done.4 = bf16[64,4,1792]{2,1,0:T(4,128)(2,1)S(1)} async-done(((bf16[64,4,1792]{2,1,0:T(4,128)(2,1)}), bf16[64,4,1792]{2,1,0:T(4,128)(2,1)S(1)}, u32[]{:S(2)}, u32[]{:S(2)}) %all-to-all-start.4) | async-done | bytes 917536 | tf_op jit(solution)/shard_map/all_to_all | solution.py:94
  326.0 0.2 reshape.126
  326.2 0.9 gather_fusion.3
  327.2 1.4 fusion.13
  (19 shorter events, 0.1 us)
Async XLA Ops:
  8.7 30.0 %all-to-all-start.2 = ((bf16[4,16,1792]{2,1,0:T(8,128)(2,1)}), bf16[4,16,1792]{2,1,0:T(8,128)(2,1)S(1)}, u32[]{:S(2)}, u32[]{:S(2)}) async-start(bf16[4,16,1792]{2,1,0:T(8,128)(2,1)} %stack.2), calls=%async_computation.3 | async-start | bytes 458752 | tf_op jit(solution)/shard_map/all_to_all | solution.py:52
  38.7 100.4 %all-to-all-start = ((bf16[64,4,7168]{2,1,0:T(4,128)(2,1)}), bf16[64,4,7168]{2,1,0:T(4,128)(2,1)}, u32[]{:S(2)}, u32[]{:S(2)}) async-start(bf16[64,4,7168]{2,1,0:T(4,128)(2,1)} %reshape.116), calls=%async_computation | async-start | bytes 7340032 | tf_op jit(solution)/shard_map/all_to_all | solution.py:61
  139.1 90.6 %all-to-all-start.3 = ((bf16[64,4,7168]{2,1,0:T(4,128)(2,1)}), bf16[64,4,7168]{2,1,0:T(4,128)(2,1)}, u32[]{:S(2)}, u32[]{:S(2)}) async-start(bf16[64,4,7168]{2,1,0:T(4,128)(2,1)} %reshape.124), calls=%async_computation.4 | async-start | bytes 7340032 | tf_op jit(solution)/shard_map/all_to_all | solution.py:62
  145.0 100.9 %reduce-scatter.3.cloned.1.call-start = ((), (), s32[]{:S(2)}) async-start(), calls=%async_computation.7 | async-start | bytes 4587520 | tf_op jit(solution)/shard_map/reduce_scatter | solution.py:80
  151.9 4.4 %copy-start = (bf16[256,7168]{1,0:T(8,128)(2,1)S(1)}, bf16[256,7168]{1,0:T(8,128)(2,1)}, u32[]{:S(2)}) copy-start(bf16[256,7168]{1,0:T(8,128)(2,1)} %reshape.117) | copy-start | bytes 11010052
  151.9 5.3 %copy-start.3 = (bf16[1,7168,256]{2,1,0:T(8,128)(2,1)S(1)}, bf16[1,7168,256]{2,1,0:T(8,128)(2,1)}, u32[]{:S(2)}) copy-start(bf16[1,7168,256]{2,1,0:T(8,128)(2,1)} %param.11) | copy-start | bytes 11010052
  157.2 2.0 copy-start.1
  162.3 124.7 %reduce-scatter.5.cloned.1.call-start = ((), (), s32[]{:S(2)}) async-start(), calls=%async_computation.8 | async-start | bytes 4587520 | tf_op jit(solution)/shard_map/reduce_scatter | solution.py:91
  236.4 4.4 %copy-start.2 = (bf16[1,7168,256]{2,1,0:T(8,128)(2,1)S(1)}, bf16[1,7168,256]{2,1,0:T(8,128)(2,1)}, u32[]{:S(2)}) copy-start(bf16[1,7168,256]{2,1,0:T(8,128)(2,1)} %param.10) | copy-start | bytes 11010052
  240.8 2.0 copy-start.4
  245.8 54.5 %copy-start.5 = (f32[16,8]{0,1:T(8,128)S(1)}, f32[16,8]{0,1:T(8,128)}, u32[]{:S(2)}) copy-start(f32[16,8]{0,1:T(8,128)} %param.9) | copy-start | bytes 1540
  248.4 41.2 %all-to-all-start.1 = ((bf16[64,4,1792]{2,1,0:T(4,128)(2,1)}), bf16[64,4,1792]{2,1,0:T(4,128)(2,1)S(1)}, u32[]{:S(2)}, u32[]{:S(2)}) async-start(bf16[64,4,1792]{2,1,0:T(4,128)(2,1)} %reshape_transpose_reshape.8), calls=%async_computation.2 | async-start | bytes 1835008 | tf_op jit(solution)/shard_map/all_to_all | solution.py:84
  289.6 36.4 %all-to-all-start.4 = ((bf16[64,4,1792]{2,1,0:T(4,128)(2,1)}), bf16[64,4,1792]{2,1,0:T(4,128)(2,1)S(1)}, u32[]{:S(2)}, u32[]{:S(2)}) async-start(bf16[64,4,1792]{2,1,0:T(4,128)(2,1)} %reshape_transpose_reshape.9), calls=%async_computation.6 | async-start | bytes 1835008 | tf_op jit(solution)/shard_map/all_to_all | solution.py:94
Sparse Core Ops, SparseCore 0:
  162.5 45.5 reduce-scatter.2
  245.9 41.0 reduce-scatter.4
